TPU v7x, 512 devices: a whole 4x4x16 slice. The times are simulated.
512 devices in a mesh: ctx: 64 (over z, x), ch: 8 (over y, core).
Axes of the slice: x: 4, y: 4, z: 16, core: 2. Of those that a mesh axis runs over, the one named last changes fastest.
Arguments:
- gate_input: bfloat16 [16384, 4096], P('ctx', 'ch'), may hold values from -6 to 6
- key_input: bfloat16 [16384, 4096], P('ctx', 'ch'), may hold values from -6 to 6
- value_input: bfloat16 [16384, 4096], P('ctx', 'ch'), may hold values from -6 to 6
- decay_rate: float32 [16, 4096], P(None, 'ch'), may hold values from 0.00012207031 to 0.26666667
- frequency: float32 [16, 4096], P(None, 'ch'), may hold values from 0 to 2.4
- residue: float32 [2, 16, 4096], P(None, None, 'ch'), may hold values from -2 to 2
- skip_gain: float32 [4096], P('ch'), may hold values from -3 to 3
- out_weight: bfloat16 [4096, 4096], P('ctx', 'ch'), may hold values from -0.09375 to 0.09375
Outputs:
- mixed: bfloat16 [16384, 4096], P('ctx', 'ch')
All inputs are finite; a program needn't handle non-finite values.
Results may differ from a plain program's by a relative error of at most 0.014.
Values may be sent and summed in bfloat16 or wider, within the bound.
A program may use at most 128 MiB of HBM per device.

v0:
```python
import jax
import jax.numpy as jnp
from jax import lax
from jax.sharding import PartitionSpec as P


def entering(value, axis, join, neutral):
    count, mine = (lax.axis_size(axis), lax.axis_index(axis))
    pieces = jax.tree.map(lambda part: lax.all_gather(part, axis), value)
    so_far = jax.tree.map(
        lambda part, zero: jnp.full_like(part, 0) + jnp.asarray(zero, part.dtype), value, neutral
    )

    def hop(position, so_far):
        longer = join(so_far, jax.tree.map(lambda part: part[position], pieces))
        return jax.tree.map(lambda new, old: jnp.where(position < mine, new, old), longer, so_far)

    return lax.fori_loop(0, count - 1, hop, so_far)


def cmul(a_re, a_im, b_re, b_im):
    return (a_re * b_re - a_im * b_im, a_re * b_im + a_im * b_re)


def filter_tables(decay_rate, frequency, residue, block_len):
    damping = 0.125 * decay_rate
    turning = 0.125 * frequency
    scaling = jnp.sqrt(2.0 * damping)
    coef_re = scaling * residue[0]
    coef_im = scaling * residue[1]
    offsets = jnp.arange(block_len).astype(jnp.float32)

    def powers(counts):
        fading = jnp.exp(-damping[None] * counts[:, None, None])
        phase = turning[None] * counts[:, None, None]
        return (fading * jnp.cos(phase), fading * jnp.sin(phase))

    back_re, back_im = powers(block_len - 1.0 - offsets)
    ahead_re, ahead_im = powers(offsets + 1.0)
    out_re, out_im = cmul(coef_re[None], coef_im[None], ahead_re, ahead_im)
    lag_re, lag_im = powers(offsets)
    filt = jnp.sum(coef_re[None] * lag_re - coef_im[None] * lag_im, axis=1)
    places = jnp.arange(block_len)
    differ = places[:, None] - places[None, :]
    picked = jnp.take(filt, jnp.maximum(differ, 0), axis=0)
    toeplitz = jnp.where((differ >= 0)[:, :, None], picked, jnp.zeros_like(picked))
    jump_re, jump_im = powers(jnp.full((1,), block_len).astype(jnp.float32))
    return (back_re, back_im, out_re, out_im, toeplitz, jump_re[0], jump_im[0])


def chain(earlier, later):
    sum_re, sum_im = cmul(earlier[0], earlier[1], later[2], later[3])
    pow_re, pow_im = cmul(earlier[2], earlier[3], later[2], later[3])
    return (sum_re + later[0], sum_im + later[1], pow_re, pow_im)


def on_device(
    gate_input, key_input, value_input, decay_rate, frequency, residue, skip_gain, out_weight
):
    highest = lax.Precision.HIGHEST
    signal = key_input.astype(jnp.float32) * value_input.astype(jnp.float32)
    tok_len, chans = signal.shape
    block_len = 16
    block_count = tok_len // block_len
    back_re, back_im, out_re, out_im, toeplitz, jump_re, jump_im = filter_tables(
        decay_rate, frequency, residue, block_len
    )
    blocks = signal.reshape(block_count, block_len, chans)
    entry_re = jnp.einsum("snc,bsc->bnc", back_re, blocks, precision=highest)
    entry_im = jnp.einsum("snc,bsc->bnc", back_im, blocks, precision=highest)

    def advance(state, entry):
        moved_re, moved_im = cmul(jump_re, jump_im, state[0], state[1])
        grown_re, grown_im = cmul(state[2], state[3], jump_re, jump_im)
        return ((moved_re + entry[0], moved_im + entry[1], grown_re, grown_im), state)

    zeros = jnp.zeros(jump_re.shape, jnp.float32)
    ones = jnp.ones(jump_re.shape, jnp.float32)
    final, starts = lax.scan(advance, (zeros, zeros, ones, zeros), (entry_re, entry_im))
    local_re, local_im, device_re, device_im = final
    prefix = entering(
        (local_re, local_im, device_re, device_im), "ctx", chain, (zeros, zeros, ones, zeros)
    )
    incoming_re, incoming_im = (prefix[0], prefix[1])
    carried_re, carried_im = cmul(starts[2], starts[3], incoming_re[None], incoming_im[None])
    begin_re = starts[0] + carried_re
    begin_im = starts[1] + carried_im
    far = jnp.einsum("tnc,bnc->btc", out_re, begin_re, precision=highest) - jnp.einsum(
        "tnc,bnc->btc", out_im, begin_im, precision=highest
    )
    near = jnp.einsum("tsc,bsc->btc", toeplitz, blocks, precision=highest)
    conv = (near + far).reshape(tok_len, chans)
    gated = (gate_input.astype(jnp.float32) * (conv + skip_gain[None, :] * signal)).astype(
        jnp.bfloat16
    )
    whole = lax.all_gather(gated, "ch", axis=1, tiled=True)
    all_rows = lax.all_gather(out_weight, "ctx", axis=0, tiled=True)
    mixed = jnp.dot(whole, all_rows, preferred_element_type=jnp.float32)
    return mixed.astype(jnp.bfloat16)


def solution(mesh):
    placed = (
        P("ctx", "ch"),
        P("ctx", "ch"),
        P("ctx", "ch"),
        P(None, "ch"),
        P(None, "ch"),
        P(None, None, "ch"),
        P("ch"),
        P("ctx", "ch"),
    )
    return jax.shard_map(
        on_device, mesh=mesh, in_specs=placed, out_specs=P("ctx", "ch"), check_vma=False
    )
```

profile of v0, /device:TPU:8, one launch (start us, length us, event | category | flops | bytes accessed | tf_op | source)
XLA Modules:
  0.0 906.5 jit_solution(10265172625318404622)
XLA Ops:
  6.6 1.1 convert_multiply_fusion
  7.7 3.7 copy.51
  11.5 6.1 multiply_add_fusion.1
  17.6 4.1 copy.54
  21.8 9.9 %convolution_bitcast_fusion.1 = f32[16,16,512]{1,0,2:T(8,128)} fusion(f32[16,16,512]{1,0,2:T(8,128)} %copy.51, f32[16,16,512]{1,0,2:T(8,128)} %copy.54), kind=kOutput, calls=%fused_computation.21 | convolution fusion | flops 25165824 | bytes 1572864 | tf_op jit(solution)/shard_map/snc,bsc->bnc/dot_general | solution.py:69
  31.7 3.5 copy.57
  35.2 3.7 copy.56
  38.9 9.9 %convolution_bitcast_fusion = f32[16,16,512]{1,0,2:T(8,128)} fusion(f32[16,16,512]{1,0,2:T(8,128)} %copy.51, f32[16,16,512]{1,0,2:T(8,128)} %copy.56), kind=kOutput, calls=%fused_computation.20 | convolution fusion | flops 25165824 | bytes 1572864 | tf_op jit(solution)/shard_map/snc,bsc->bnc/dot_general | solution.py:70
  48.8 3.5 copy.58
  52.5 14.0 %while.41 = (s32[]{:T(128)}, f32[16,512]{1,0:T(8,128)S(1)}, f32[16,512]{1,0:T(8,128)S(1)}, f32[16,512]{1,0:T(8,128)S(1)}, f32[16,512]{1,0:T(8,128)S(1)}, /*index...) while((s32[]{:T(128)}, f32[16,512]{1,0:T(8,128)S(1)}, ...), condition=%wide.region_2.3_spmd.clone, body=%wide.region_1.2_spmd.clone.sunk | while | flops 180227 | bytes 655533 | solution.py:79
  69.6 1.8 gather_fusion
  71.4 2.0 select_select_fusion
  73.4 4.5 copy.52
  77.9 3.6 copy.60
  81.5 3.7 copy.62
  85.2 12.3 %fusion.17 = f32[512,16,16]{2,1,0:T(8,128)} fusion(f32[16,16,512]{1,0,2:T(8,128)} %copy.51, f32[16,16,512]{1,0,2:T(8,128)} %copy.52), kind=kOutput, calls=%fused_computation.66 | convolution fusion | flops 25165824 | bytes 1572864 | tf_op jit(solution)/shard_map/tsc,bsc->btc/dot_general | solution.py:91
  97.5 115.2 %all-gather.15.cloned.1.call-done = f32[1024,512]{1,0:T(8,128)} async-done(((f32[16,512]{1,0:T(8,128)}), f32[1024,512]{1,0:T(8,128)}) %all-gather.15.cloned.1.call-update) | async-done | bytes 2097168 | tf_op jit(solution)/shard_map/all_gather | solution.py:9
  212.7 139.9 %all-gather.17.cloned.1.call-done = f32[1024,512]{1,0:T(8,128)} async-done(((f32[16,512]{1,0:T(8,128)}), f32[1024,512]{1,0:T(8,128)}) %all-gather.17.cloned.1.call-update) | async-done | bytes 2097168 | tf_op jit(solution)/shard_map/all_gather | solution.py:9
  352.6 139.9 %all-gather.19.cloned.1.call-done = f32[1024,512]{1,0:T(8,128)} async-done(((f32[16,512]{1,0:T(8,128)}), f32[1024,512]{1,0:T(8,128)}) %all-gather.19.cloned.1.call-update) | async-done | bytes 2097168 | tf_op jit(solution)/shard_map/all_gather | solution.py:9
  492.5 139.8 %all-gather.21.cloned.1.call-done = f32[1024,512]{1,0:T(8,128)} async-done(((f32[16,512]{1,0:T(8,128)}), f32[1024,512]{1,0:T(8,128)}) %all-gather.21.cloned.1.call-update) | async-done | bytes 2097168 | tf_op jit(solution)/shard_map/all_gather | solution.py:9
  632.3 54.2 %while.42 = (s32[]{:T(128)}, f32[16,512]{1,0:T(8,128)S(1)}, f32[16,512]{1,0:T(8,128)S(1)}, s32[]{:T(128)}, f32[64,16,512]{2,1,0:T(8,128)}, /*index=5*/f32[64,16,...) while((s32[]{:T(128)}, f32[16,512]{1,0:T(8,128)S(1)}, ...), condition=%wide.region_4.5_spmd.clone, body=%wide.region_3.4_spmd.clone.sunk | while | flops 98308 | bytes 262277 | solution.py:18
  643.5 0.9 fusion.32
  644.3 0.8 fusion.32
  645.2 0.8 fusion.32
  646.1 0.8 fusion.32
  646.9 0.8 fusion.32
  647.8 0.8 fusion.32
  648.6 0.8 fusion.32
  649.5 0.8 fusion.32
  650.4 0.8 fusion.32
  651.2 0.8 fusion.32
  652.1 0.8 fusion.32
  652.9 0.8 fusion.32
  653.8 0.8 fusion.32
  654.7 0.8 fusion.32
  655.5 0.8 fusion.32
  656.4 0.8 fusion.32
  657.2 0.8 fusion.32
  658.1 0.8 fusion.32
  686.8 3.7 copy.59
  690.4 3.6 copy.61
  694.1 9.5 %fusion.18 = f32[512,16,16]{2,1,0:T(8,128)S(1)} fusion(f32[16,16,512]{1,0,2:T(8,128)} %copy.59, f32[16,16,512]{1,0,2:T(8,128)} %copy.60), kind=kOutput, calls=%fused_computation.67 | convolution fusion | flops 25165824 | bytes 1572864 | tf_op jit(solution)/shard_map/tnc,bnc->btc/dot_general | solution.py:88
  703.6 8.5 add_bitcast_fusion
  712.1 2.9 copy.63
  715.0 0.8 fusion.15
  716.5 27.5 %all-gather.11.cloned.1.call-done = bf16[256,4096]{1,0:T(8,128)(2,1)} async-done(((bf16[256,512]{1,0:T(8,128)(2,1)}), bf16[256,4096]{1,0:T(8,128)(2,1)}) %all-gather.11.cloned.1.call-update) | async-done | bytes 2097168 | tf_op jit(solution)/shard_map/all_gather | solution.py:96
  744.0 150.7 %all-gather.13.cloned.1.call-done = bf16[4096,512]{1,0:T(8,128)(2,1)} async-done(((bf16[64,512]{1,0:T(8,128)(2,1)}), bf16[4096,512]{1,0:T(8,128)(2,1)}) %all-gather.13.cloned.1.call-update) | async-done | bytes 4194320 | tf_op jit(solution)/shard_map/all_gather | solution.py:97
  894.6 4.8 convolution_convert_fusion
  (151 shorter events, 55.3 us)
Async XLA Ops:
  6.5 4.8 copy-start.11
  6.5 4.8 copy-start.12
  6.5 4.8 copy-start.10
  6.5 206.1 %all-gather.15.cloned.1.call-start = ((), (), s32[]{:S(2)}) async-start(), calls=%async_computation.2 | async-start | bytes 2129920 | tf_op jit(solution)/shard_map/all_gather | solution.py:9
  66.5 0.6 copy-start.5
  66.6 0.7 copy-start.6
  66.6 1.4 copy-start.3
  66.6 2.1 copy-start.4
  67.2 285.4 %all-gather.17.cloned.1.call-start = ((), (), s32[]{:S(2)}) async-start(), calls=%async_computation.3 | async-start | bytes 2129920 | tf_op jit(solution)/shard_map/all_gather | solution.py:9
  67.9 424.6 %all-gather.19.cloned.1.call-start = ((), (), s32[]{:S(2)}) async-start(), calls=%async_computation.4 | async-start | bytes 2129920 | tf_op jit(solution)/shard_map/all_gather | solution.py:9
  68.7 563.6 %all-gather.21.cloned.1.call-start = ((), (), s32[]{:S(2)}) async-start(), calls=%async_computation.5 | async-start | bytes 2129920 | tf_op jit(solution)/shard_map/all_gather | solution.py:9
  69.2 674.7 %all-gather.11.cloned.1.call-start = ((), (), s32[]{:S(2)}) async-start(), calls=%async_computation | async-start | bytes 2359296 | tf_op jit(solution)/shard_map/all_gather | solution.py:96
  694.1 9.5 %copy-start = (f32[512,16,16]{2,1,0:T(8,128)S(1)}, f32[512,16,16]{2,1,0:T(8,128)}, u32[]{:S(2)}) copy-start(f32[512,16,16]{2,1,0:T(8,128)} %fusion.17) | copy-start | bytes 1572868
  694.1 9.5 %copy-start.1 = (f32[16,16,512]{1,0,2:T(8,128)S(1)}, f32[16,16,512]{1,0,2:T(8,128)}, u32[]{:S(2)}) copy-start(f32[16,16,512]{1,0,2:T(8,128)} %copy.62) | copy-start | bytes 1572868
  694.1 9.5 %copy-start.2 = (f32[16,16,512]{1,0,2:T(8,128)S(1)}, f32[16,16,512]{1,0,2:T(8,128)}, u32[]{:S(2)}) copy-start(f32[16,16,512]{1,0,2:T(8,128)} %copy.61) | copy-start | bytes 1572868
  712.1 2.9 copy-start.7
  712.1 2.9 copy-start.8
  712.1 2.9 copy-start.9
  712.1 2.9 copy-start.13
  715.9 178.7 %all-gather.13.cloned.1.call-start = ((), (), s32[]{:S(2)}) async-start(), calls=%async_computation.1 | async-start | bytes 4259840 | tf_op jit(solution)/shard_map/all_gather | solution.py:97
Sparse Core Ops, SparseCore 0:
  67.3 145.3 all-gather.14
  215.6 136.9 all-gather.16
  355.5 136.9 all-gather.18
  495.3 136.9 all-gather.20
  716.0 27.8 all-gather.10
  746.8 147.8 all-gather.12
where the time goes:
time: 918 us; the launch traced here: 906 us
  waiting for transfers between devices  715 us (78%)
  other arithmetic  76.7 us (8%)
  matrix products  54.8 us (6%)
  local copies, waits for them, and re-layouts  43.3 us (5%)
  between operations  14 us (2%)
    all_gather x4, waiting for transfers between devices, entering(): pieces = jax.tree.map(lambda part: lax.all_gather(part, axis), value)  535 us
    all_gather x1, waiting for transfers between devices, on_device(): all_rows = lax.all_gather(out_weight, 'ctx', axis=0, tiled=True)  151 us
    select_n x63, other arithmetic, hop(): jnp.where(position < mine, new, old)  52.8 us
    all_gather x1, waiting for transfers between devices, on_device(): whole = lax.all_gather(gated, 'ch', axis=1, tiled=True)  27.5 us
    add x17, other arithmetic, cmul(): return (a_re * b_re - a_im * b_im, a_re * b_im + a_im * b_re)  19.1 us
  transfers between devices with their start and end apart: 6, of which 6 were waited for; matrix products, arithmetic and copies ran while one was open for 3% of the time, Pallas kernels for 0%

commit v1 on v0

--- a/solution.py
+++ b/solution.py
@@ -94,7 +94,8 @@
         jnp.bfloat16
     )
     whole = lax.all_gather(gated, "ch", axis=1, tiled=True)
-    all_rows = lax.all_gather(out_weight, "ctx", axis=0, tiled=True)
+    sent = jnp.stack([out_weight] * lax.axis_size("ctx"))
+    all_rows = jnp.concatenate(lax.all_to_all(sent, "ctx", 0, 0), axis=0)
     mixed = jnp.dot(whole, all_rows, preferred_element_type=jnp.float32)
     return mixed.astype(jnp.bfloat16)
 

time: 918 us -> 824 us (0.90)
  the two profiles are of different devices: /device:TPU:8 before, /device:TPU:1 now
where the time goes in v1:
time: 824 us; the launch traced here: 812 us
  waiting for transfers between devices  599 us (73%)
  other arithmetic  76.9 us (9%)
  matrix products  54.7 us (7%)
  local copies, waits for them, and re-layouts  46 us (6%)
  starting transfers between devices  19.7 us (2%)
  between operations  13.7 us (2%)
    all_gather x4, waiting for transfers between devices, entering(): pieces = jax.tree.map(lambda part: lax.all_gather(part, axis), value)  559 us
    select_n x63, other arithmetic, hop(): jnp.where(position < mine, new, old)  52.9 us
    all_gather x1, waiting for transfers between devices, on_device(): whole = lax.all_gather(gated, 'ch', axis=1, tiled=True)  38.3 us
    all_to_all x1, starting transfers between devices, on_device(): all_rows = jnp.concatenate(lax.all_to_all(sent, 'ctx', 0, 0), axis=0)  19.5 us
    add x17, other arithmetic, cmul(): return (a_re * b_re - a_im * b_im, a_re * b_im + a_im * b_re)  19.1 us
  transfers between devices with their start and end apart: 6, of which 5 were waited for; matrix products, arithmetic and copies ran while one was open for 14% of the time, Pallas kernels for 0%

profile of v1, /device:TPU:1, one launch (start us, length us, event | category | flops | bytes accessed | tf_op | source)
XLA Modules:
  0.0 812.4 jit_solution(11786041323372526939)
XLA Ops:
  6.6 1.1 convert_multiply_fusion
  7.7 3.7 copy.51
  11.6 6.1 multiply_add_fusion.1
  17.7 4.2 copy.54
  21.8 9.9 %convolution_bitcast_fusion.1 = f32[16,16,512]{1,0,2:T(8,128)} fusion(f32[16,16,512]{1,0,2:T(8,128)} %copy.51, f32[16,16,512]{1,0,2:T(8,128)} %copy.54), kind=kOutput, calls=%fused_computation.21 | convolution fusion | flops 25165824 | bytes 1572864 | tf_op jit(solution)/shard_map/snc,bsc->bnc/dot_general | solution.py:69
  31.7 3.5 copy.57
  35.2 3.7 copy.56
  38.9 9.9 %convolution_bitcast_fusion = f32[16,16,512]{1,0,2:T(8,128)} fusion(f32[16,16,512]{1,0,2:T(8,128)} %copy.51, f32[16,16,512]{1,0,2:T(8,128)} %copy.56), kind=kOutput, calls=%fused_computation.20 | convolution fusion | flops 25165824 | bytes 1572864 | tf_op jit(solution)/shard_map/snc,bsc->bnc/dot_general | solution.py:70
  48.8 3.5 copy.58
  52.5 14.0 %while.41 = (s32[]{:T(128)}, f32[16,512]{1,0:T(8,128)S(1)}, f32[16,512]{1,0:T(8,128)S(1)}, f32[16,512]{1,0:T(8,128)S(1)}, f32[16,512]{1,0:T(8,128)S(1)}, /*index...) while((s32[]{:T(128)}, f32[16,512]{1,0:T(8,128)S(1)}, ...), condition=%wide.region_2.3_spmd.clone, body=%wide.region_1.2_spmd.clone.sunk | while | flops 180227 | bytes 655533 | solution.py:79
  69.3 2.5 stack.2
  71.8 19.5 %all-to-all-start = ((bf16[64,64,512]{2,1,0:T(8,128)(2,1)}), bf16[64,64,512]{2,1,0:T(8,128)(2,1)}, u32[]{:S(2)}, u32[]{:S(2)}) async-start(bf16[64,64,512]{2,1,0:T(8,128)(2,1)} %stack.2), calls=%async_computation | async-start | bytes 8388608 | tf_op jit(solution)/shard_map/all_to_all | solution.py:98
  91.5 1.8 gather_fusion
  93.3 2.0 select_select_fusion
  95.3 4.6 copy.52
  99.9 3.7 copy.60
  103.6 3.6 copy.62
  107.2 12.2 %fusion.17 = f32[512,16,16]{2,1,0:T(8,128)} fusion(f32[16,16,512]{1,0,2:T(8,128)} %copy.51, f32[16,16,512]{1,0,2:T(8,128)} %copy.52), kind=kOutput, calls=%fused_computation.66 | convolution fusion | flops 25165824 | bytes 1572864 | tf_op jit(solution)/shard_map/tsc,bsc->btc/dot_general | solution.py:91
  119.4 148.7 %all-gather.12.cloned.1.call-done = f32[1024,512]{1,0:T(8,128)} async-done(((f32[16,512]{1,0:T(8,128)}), f32[1024,512]{1,0:T(8,128)}) %all-gather.12.cloned.1.call-update) | async-done | bytes 2097168 | tf_op jit(solution)/shard_map/all_gather | solution.py:9
  268.1 130.9 %all-gather.14.cloned.1.call-done = f32[1024,512]{1,0:T(8,128)} async-done(((f32[16,512]{1,0:T(8,128)}), f32[1024,512]{1,0:T(8,128)}) %all-gather.14.cloned.1.call-update) | async-done | bytes 2097168 | tf_op jit(solution)/shard_map/all_gather | solution.py:9
  399.0 139.9 %all-gather.16.cloned.1.call-done = f32[1024,512]{1,0:T(8,128)} async-done(((f32[16,512]{1,0:T(8,128)}), f32[1024,512]{1,0:T(8,128)}) %all-gather.16.cloned.1.call-update) | async-done | bytes 2097168 | tf_op jit(solution)/shard_map/all_gather | solution.py:9
  538.9 139.8 %all-gather.18.cloned.1.call-done = f32[1024,512]{1,0:T(8,128)} async-done(((f32[16,512]{1,0:T(8,128)}), f32[1024,512]{1,0:T(8,128)}) %all-gather.18.cloned.1.call-update) | async-done | bytes 2097168 | tf_op jit(solution)/shard_map/all_gather | solution.py:9
  678.7 54.3 %while.42 = (s32[]{:T(128)}, f32[16,512]{1,0:T(8,128)S(1)}, f32[16,512]{1,0:T(8,128)S(1)}, s32[]{:T(128)}, f32[64,16,512]{2,1,0:T(8,128)}, /*index=5*/f32[64,16,...) while((s32[]{:T(128)}, f32[16,512]{1,0:T(8,128)S(1)}, ...), condition=%wide.region_4.5_spmd.clone, body=%wide.region_3.4_spmd.clone.sunk | while | flops 98308 | bytes 262277 | solution.py:18
  679.5 0.8 fusion.32
  680.4 0.8 fusion.32
  681.2 0.8 fusion.32
  685.5 0.9 fusion.32
  687.3 0.9 fusion.32
  696.8 0.9 fusion.32
  698.5 0.8 fusion.32
  705.4 0.8 fusion.32
  706.3 0.8 fusion.32
  707.1 0.8 fusion.32
  710.6 0.8 fusion.32
  712.3 0.8 fusion.32
  713.1 0.9 fusion.32
  716.6 0.8 fusion.32
  719.2 0.9 fusion.32
  726.1 0.8 fusion.32
  727.0 0.8 fusion.32
  733.3 3.7 copy.59
  737.0 3.7 copy.61
  740.7 9.5 %fusion.18 = f32[512,16,16]{2,1,0:T(8,128)S(1)} fusion(f32[16,16,512]{1,0,2:T(8,128)} %copy.59, f32[16,16,512]{1,0,2:T(8,128)} %copy.60), kind=kOutput, calls=%fused_computation.67 | convolution fusion | flops 25165824 | bytes 1572864 | tf_op jit(solution)/shard_map/tnc,bnc->btc/dot_general | solution.py:88
  750.2 8.6 %add_bitcast_fusion = f32[16,16,512]{1,0,2:T(8,128)} fusion(f32[512,16,16]{2,1,0:T(8,128)S(1)} %copy-done, f32[512,16,16]{2,1,0:T(8,128)S(1)} %fusion.18, f32[16,16,512]{1,0,2:T(8,128)S(1)} %copy-done.2, f32[16,16,512]{1,0,2:T(8,128)S(1)} %copy-done.1), kind=kOutput, calls=%fused_computation.19 | convolution fusion | flops 25427968 | bytes 2621440 | tf_op jit(solution)/shard_map/tnc,bnc->btc/dot_general | solution.py:88
  758.7 2.9 copy.63
  761.7 0.8 fusion.15
  762.5 38.3 %all-gather.10.cloned.1.call-done = bf16[256,4096]{1,0:T(8,128)(2,1)} async-done(((bf16[256,512]{1,0:T(8,128)(2,1)}), bf16[256,4096]{1,0:T(8,128)(2,1)}) %all-gather.10.cloned.1.call-update) | async-done | bytes 2097168 | tf_op jit(solution)/shard_map/all_gather | solution.py:96
  800.8 4.8 convolution_convert_fusion
  (153 shorter events, 55.5 us)
Async XLA Ops:
  6.5 4.9 copy-start.12
  6.5 4.9 copy-start.13
  6.5 4.9 copy-start.11
  6.5 261.6 %all-gather.12.cloned.1.call-start = ((), (), s32[]{:S(2)}) async-start(), calls=%async_computation.2 | async-start | bytes 2129920 | tf_op jit(solution)/shard_map/all_gather | solution.py:9
  48.8 20.5 %copy-start.10 = (bf16[64,512]{1,0:T(8,128)(2,1)S(1)}, bf16[64,512]{1,0:T(8,128)(2,1)}, u32[]{:S(2)}) copy-start(bf16[64,512]{1,0:T(8,128)(2,1)} %param.19) | copy-start | bytes 196612
  66.5 0.6 copy-start.5
  66.6 0.7 copy-start.6
  66.6 1.4 copy-start.3
  66.6 2.1 copy-start.4
  67.2 331.8 %all-gather.14.cloned.1.call-start = ((), (), s32[]{:S(2)}) async-start(), calls=%async_computation.3 | async-start | bytes 2129920 | tf_op jit(solution)/shard_map/all_gather | solution.py:9
  67.9 471.0 %all-gather.16.cloned.1.call-start = ((), (), s32[]{:S(2)}) async-start(), calls=%async_computation.4 | async-start | bytes 2129920 | tf_op jit(solution)/shard_map/all_gather | solution.py:9
  68.7 610.0 %all-gather.18.cloned.1.call-start = ((), (), s32[]{:S(2)}) async-start(), calls=%async_computation.5 | async-start | bytes 2129920 | tf_op jit(solution)/shard_map/all_gather | solution.py:9
  71.8 729.0 %all-to-all-start = ((bf16[64,64,512]{2,1,0:T(8,128)(2,1)}), bf16[64,64,512]{2,1,0:T(8,128)(2,1)}, u32[]{:S(2)}, u32[]{:S(2)}) async-start(bf16[64,64,512]{2,1,0:T(8,128)(2,1)} %stack.2), calls=%async_computation | async-start | bytes 8388608 | tf_op jit(solution)/shard_map/all_to_all | solution.py:98
  91.3 709.5 %all-gather.10.cloned.1.call-start = ((), (), s32[]{:S(2)}) async-start(), calls=%async_computation.1 | async-start | bytes 2359296 | tf_op jit(solution)/shard_map/all_gather | solution.py:96
  740.7 9.5 %copy-start = (f32[512,16,16]{2,1,0:T(8,128)S(1)}, f32[512,16,16]{2,1,0:T(8,128)}, u32[]{:S(2)}) copy-start(f32[512,16,16]{2,1,0:T(8,128)} %fusion.17) | copy-start | bytes 1572868
  740.7 9.5 %copy-start.1 = (f32[16,16,512]{1,0,2:T(8,128)S(1)}, f32[16,16,512]{1,0,2:T(8,128)}, u32[]{:S(2)}) copy-start(f32[16,16,512]{1,0,2:T(8,128)} %copy.62) | copy-start | bytes 1572868
  740.7 9.5 %copy-start.2 = (f32[16,16,512]{1,0,2:T(8,128)S(1)}, f32[16,16,512]{1,0,2:T(8,128)}, u32[]{:S(2)}) copy-start(f32[16,16,512]{1,0,2:T(8,128)} %copy.61) | copy-start | bytes 1572868
  758.7 2.9 copy-start.7
  758.7 2.9 copy-start.8
  758.7 2.9 copy-start.9
  758.7 2.9 copy-start.14
Sparse Core Ops, SparseCore 0:
  67.3 200.7 all-gather.11
  271.1 127.8 all-gather.13
  401.9 136.9 all-gather.15
  541.7 136.9 all-gather.17
  762.6 38.1 all-gather.9
